TPU v7x, 32 devices: a whole 2x2x4 slice. The times are simulated.
32 devices in a mesh: row: 4 (over y, x), col: 8 (over z, core).
Axes of the slice: x: 2, y: 2, z: 4, core: 2. Of those that a mesh axis runs over, the one named last changes fastest.
Arguments:
- trailing_grad: bfloat16 [4, 8, 768, 24576], P(None, 'col', None, 'row'), may hold values from -6 to 6
- panel: bfloat16 [24576, 512], P(('row', 'col')), may hold values from -0.0390625 to 0.0390625
- panel_grad: float32 [24576, 512], P(('row', 'col')), may hold values from -6 to 6
- diag_factor: float32 [512, 512], replicated, may hold values from -2 to 2, as said below
- diag_grad: float32 [512, 512], replicated, may hold values from -6 to 6
Outputs:
- panel_adj: float32 [24576, 512], P(('row', 'col'))
- diag_adj: float32 [512, 512], replicated
Inputs may be any that keep to these rules, and one draw needn't show every extreme that they name: `diag_factor`: lower triangular with zeros above the diagonal; diagonal entries between 1 and 2.
All inputs are finite; a program needn't handle non-finite values.
Results may differ from a plain program's by a relative error of at most 0.0003.
Values may be sent and summed in bfloat16 or wider, within the bound.
A program may use at most 128 MiB of HBM per device.

v0:
```python
import jax
import jax.numpy as jnp
from jax import lax
from jax.sharding import PartitionSpec as P


def halve_lower(matrix):
    rows = lax.broadcasted_iota(jnp.int32, matrix.shape, 0)
    cols = lax.broadcasted_iota(jnp.int32, matrix.shape, 1)
    keep = jnp.where(rows > cols, 1.0, jnp.where(rows == cols, 0.5, 0.0)).astype(jnp.float32)
    return matrix * keep


def keep_lower(matrix):
    rows = lax.broadcasted_iota(jnp.int32, matrix.shape, 0)
    cols = lax.broadcasted_iota(jnp.int32, matrix.shape, 1)
    return jnp.where(rows >= cols, matrix, 0.0)


def right_solve(left, lower):
    right = jax.scipy.linalg.solve_triangular(lower, left.T, lower=True, trans=1).T
    return 0.5 * (right + right.T)


def on_device(trailing_grad, panel, panel_grad, diag_factor, diag_grad):
    local_flip = trailing_grad.reshape(-1, trailing_grad.shape[3])
    lower = jnp.tril(diag_factor)
    col_panel = lax.all_gather(panel, "row", axis=0, tiled=True)
    row_panel = lax.all_gather(panel, "col", axis=0, tiled=True)
    block = local_flip
    direct = lax.psum_scatter(
        lax.dot_general(
            block, col_panel, (((0,), (0,)), ((), ())), preferred_element_type=jnp.float32
        ),
        "col",
        scatter_dimension=0,
        tiled=True,
    )
    block = local_flip
    transposed = lax.psum_scatter(
        jnp.dot(block, row_panel, preferred_element_type=jnp.float32),
        "row",
        scatter_dimension=0,
        tiled=True,
    )
    reduced = panel_grad - direct - transposed
    panel_adj = jax.scipy.linalg.solve_triangular(lower, reduced.T, lower=True, trans=1).T
    contrib = lax.dot_general(
        panel_adj,
        panel.astype(jnp.float32),
        (((0,), (0,)), ((), ())),
        precision=lax.Precision.HIGHEST,
    )
    diag_new = diag_grad - lax.psum(contrib, ("row", "col"))
    inner = halve_lower(jnp.dot(lower.T, keep_lower(diag_new), precision=lax.Precision.HIGHEST))
    left = jax.scipy.linalg.solve_triangular(lower, inner, lower=True, trans=1)
    return (panel_adj, right_solve(left, lower))


def solution(mesh):
    in_specs = (
        P(None, "col", None, "row"),
        P(("row", "col"), None),
        P(("row", "col"), None),
        P(),
        P(),
    )
    out_specs = (P(("row", "col"), None), P())
    return jax.shard_map(
        on_device, mesh=mesh, in_specs=in_specs, out_specs=out_specs, check_vma=False
    )
```

profile of v0, /device:TPU:0, one launch (start us, length us, event | category | flops | bytes accessed | tf_op | source)
XLA Modules:
  0.0 489.1 jit_solution(2284740775558172705)
XLA Ops:
  8.7 68.4 %all-gather.5.cloned.1.call-done = bf16[6144,512]{1,0:T(8,128)(2,1)} async-done(((bf16[768,512]{1,0:T(8,128)(2,1)}), bf16[6144,512]{1,0:T(8,128)(2,1)}) %all-gather.5.cloned.1.call-update) | async-done | bytes 6291472 | tf_op jit(solution)/shard_map/all_gather | solution.py:29
  77.1 26.8 %fusion.67 = f32[3072,512]{1,0:T(8,128)} fusion(bf16[3072,6144]{1,0:T(8,128)(2,1)} %bitcast.70, bf16[6144,512]{1,0:T(8,128)(2,1)} %all-gather.5.cloned.1.call-done), kind=kOutput, calls=%fused_computation.91 | convolution fusion | flops 19327352832 | bytes 50331648 | tf_op jit(solution)/shard_map/dot_general | solution.py:41
  103.9 17.5 %all-gather.3.cloned.1.call-done = bf16[3072,512]{1,0:T(8,128)(2,1)} async-done(((bf16[768,512]{1,0:T(8,128)(2,1)}), bf16[3072,512]{1,0:T(8,128)(2,1)}) %all-gather.3.cloned.1.call-update) | async-done | bytes 3145744 | tf_op jit(solution)/shard_map/all_gather | solution.py:28
  121.4 27.7 %fusion.66 = f32[6144,512]{1,0:T(8,128)} fusion(bf16[3072,6144]{1,0:T(8,128)(2,1)} %bitcast.71, bf16[3072,512]{1,0:T(8,128)(2,1)} %all-gather.3.cloned.1.call-done), kind=kOutput, calls=%fused_computation.90 | convolution fusion | flops 19327352832 | bytes 53477376 | tf_op jit(solution)/shard_map/dot_general | solution.py:32
  149.2 1.1 copy-done.6
  150.5 8.0 %while.5 = (s32[]{:T(128)}, f32[512,512]{1,0:T(8,128)S(1)}, s32[4,2]{0,1:T(2,128)S(1)}, f32[4,128,128]{2,1,0:T(8,128)S(1)}, s32[]{:T(128)}) while((s32[]{:T(128)}, f32[512,512]{1,0:T(8,128)S(1)}, s32[4,2]{0,1:T(2,128)S(1)}, f32[4,128,128]{2,1,0:T(8,128)S(1)}, s32[]{:T(128)}) %tuple.32), condition=%wide.while_cond.1, body=%wide.while_body.1.sunk | while | flops 2 | bytes 131181 | solution.py:47
  151.1 1.4 bitcast_dynamic-update-slice_fusion.2
  153.1 1.3 bitcast_dynamic-update-slice_fusion.2
  155.1 1.3 bitcast_dynamic-update-slice_fusion.2
  157.1 1.3 bitcast_dynamic-update-slice_fusion.2
  158.5 39.5 %custom-call.7 = f32[4,128,128]{1,2,0:T(8,128)S(1)} custom-call(f32[4,128,128]{2,1,0:T(8,128)S(1)} %get-tuple-element.18), custom_call_target="InvertDiagBlocksLowerTriangular" | custom-call | tf_op jit(solution)/shard_map/jit(_solve_triangular)/triangular_solve | solution.py:47
  198.0 127.9 %reduce-scatter.3.cloned.1.call-done = f32[768,512]{1,0:T(8,128)} async-done(((f32[6144,512]{1,0:T(8,128)}), f32[768,512]{1,0:T(8,128)}) %reduce-scatter.3.cloned.1.call-update) | async-done | bytes 1572880 | tf_op jit(solution)/shard_map/reduce_scatter | solution.py:31
  325.9 2.9 subtract_bitcast_fusion
  330.6 1.4 convolution_subtract_fusion.2
  332.5 2.1 convolution_subtract_fusion
  334.7 1.2 fusion.47
  335.9 3.4 fusion.10
  339.3 1.2 fusion.11
  340.5 1.6 copy.8
  342.2 126.4 %all-reduce.2.cloned.1.call-done = f32[512,512]{1,0:T(8,128)} async-done(((f32[512,512]{1,0:T(8,128)}), f32[512,512]{1,0:T(8,128)}) %all-reduce.2.cloned.1.call-update) | async-done | bytes 1048592 | tf_op jit(solution)/shard_map/psum | solution.py:54
  468.6 3.7 convolution_multiply_fusion
  477.1 1.0 convolution_subtract_fusion.3
  478.5 1.5 convolution_subtract_fusion.7
  481.4 1.2 add_multiply_fusion
  (55 shorter events, 12.9 us)
Async XLA Ops:
  7.2 69.9 %all-gather.5.cloned.1.call-start = ((), (), s32[]{:S(2)}) async-start(), calls=%async_computation.4 | async-start | bytes 7077888 | tf_op jit(solution)/shard_map/all_gather | solution.py:29
  7.9 113.5 %all-gather.3.cloned.1.call-start = ((), (), s32[]{:S(2)}) async-start(), calls=%async_computation.2 | async-start | bytes 3932160 | tf_op jit(solution)/shard_map/all_gather | solution.py:28
  8.6 189.3 %reduce-scatter.5.cloned.1.call-start = ((), (), s32[]{:S(2)}) async-start(), calls=%async_computation.5 | async-start | bytes 7864320 | tf_op jit(solution)/shard_map/reduce_scatter | solution.py:40
  103.8 222.1 %reduce-scatter.3.cloned.1.call-start = ((), (), s32[]{:S(2)}) async-start(), calls=%async_computation.3 | async-start | bytes 14155776 | tf_op jit(solution)/shard_map/reduce_scatter | solution.py:31
  149.1 1.2 copy-start.6
  149.1 319.4 %all-reduce.2.cloned.1.call-start = ((), (), s32[]{:S(2)}) async-start(), calls=%async_computation.6 | async-start | bytes 2097152 | tf_op jit(solution)/shard_map/psum | solution.py:54
  198.0 136.7 %copy-start.4 = (f32[4,128,128]{1,2,0:T(8,128)}, f32[4,128,128]{1,2,0:T(8,128)S(1)}, u32[]{:S(2)}) copy-start(f32[4,128,128]{1,2,0:T(8,128)S(1)} %custom-call.7) | copy-start | bytes 786436
  332.5 3.4 copy-start.2
  332.5 3.4 copy-start.3
  342.2 130.1 %copy-start.5 = (f32[4,128,128]{1,2,0:T(8,128)S(1)}, f32[4,128,128]{1,2,0:T(8,128)}, u32[]{:S(2)}) copy-start(f32[4,128,128]{1,2,0:T(8,128)} %copy-done.4) | copy-start | bytes 786436
  478.4 1.9 copy-start
  480.4 1.0 copy-start.1
Sparse Core Ops, SparseCore 0:
  9.6 67.4 all-gather.4
  78.9 42.4 all-gather.2
  124.4 70.1 reduce-scatter.4
  196.8 129.1 reduce-scatter.2
  339.4 129.0 all-reduce.1
where the time goes:
time: 489 us
  waiting for transfers between devices  342 us (70%)
  matrix products  76.4 us (16%)
  other arithmetic  45.1 us (9%)
  between operations  14.1 us (3%)
  local copies, waits for them, and re-layouts  11.6 us (2%)
    reduce_scatter x1, waiting for transfers between devices, on_device(): lax.psum_scatter(lax.dot_general(block, col_panel, (((0,), (0,)), ((), ()...  128 us
    psum x1, waiting for transfers between devices, on_device(): diag_new = diag_grad - lax.psum(contrib, ('row', 'col'))  126 us
    all_gather x1, waiting for transfers between devices, on_device(): row_panel = lax.all_gather(panel, 'col', axis=0, tiled=True)  68.4 us
    another operation x3, other arithmetic, on_device(): jax.scipy.linalg.solve_triangular(lower, reduced.T, lower=True, trans=1)  39.6 us
    dot_general x1, matrix products, on_device(): lax.dot_general(block, col_panel, (((0,), (0,)), ((), ())), preferred_ele...  27.7 us
    dot_general x1, matrix products, on_device(): jnp.dot(block, row_panel, preferred_element_type=jnp.float32)  26.8 us
    all_gather x1, waiting for transfers between devices, on_device(): col_panel = lax.all_gather(panel, 'row', axis=0, tiled=True)  17.5 us
  transfers between devices with their start and end apart: 5, of which 4 were waited for; matrix products, arithmetic and copies ran while one was open for 21% of the time, Pallas kernels for 0%

commit v1 on v0

--- a/solution.py
+++ b/solution.py
@@ -26,7 +26,10 @@
     local_flip = trailing_grad.reshape(-1, trailing_grad.shape[3])
     lower = jnp.tril(diag_factor)
     col_panel = lax.all_gather(panel, "row", axis=0, tiled=True)
-    row_panel = lax.all_gather(panel, "col", axis=0, tiled=True)
+    size = lax.axis_size("col")
+    shards = jnp.stack([panel for _ in range(size)])
+    shards = lax.all_to_all(shards, "col", split_axis=0, concat_axis=0)
+    row_panel = jnp.concatenate(shards, axis=0)
     block = local_flip
     direct = lax.psum_scatter(
         lax.dot_general(

time: 489 us -> 547 us (1.12)
  waiting for transfers between devices: 342 us -> 390 us
  starting transfers between devices: 0.2 us -> 6.51 us
    all_to_all x0 -> x1, waiting for transfers between devices: none -> 138 us  [on_device(): shards = lax.all_to_all(shards, 'col', split_axis=0, concat_axis=0)]
    all_gather x1 -> x0, waiting for transfers between devices: 68.4 us -> none  [on_device(): row_panel = lax.all_gather(panel, 'col', axis=0, tiled=True)]
    all_gather x1, waiting for transfers between devices: 17.5 us -> 0.02 us  [on_device(): col_panel = lax.all_gather(panel, 'row', axis=0, tiled=True)]
    all_to_all x0 -> x1, starting transfers between devices: none -> 6.35 us  [on_device(): shards = lax.all_to_all(shards, 'col', split_axis=0, concat_axis=0)]
    another operation x12 -> x13, local copies, waits for them, and re-layouts: 7.88 us -> 12.2 us
  transfers between devices with their start and end apart: 5 -> 5, of which waited for: 4 -> 3; matrix products, arithmetic and copies ran while one was open for 21% -> 19% of each run, Pallas kernels for 0% -> 0%
where the time goes in v1:
time: 547 us
  waiting for transfers between devices  390 us (71%)
  matrix products  74.6 us (14%)
  other arithmetic  45.1 us (8%)
  local copies, waits for them, and re-layouts  16.7 us (3%)
  between operations  14.1 us (3%)
  starting transfers between devices  6.51 us (1%)
    all_to_all x1, waiting for transfers between devices, on_device(): shards = lax.all_to_all(shards, 'col', split_axis=0, concat_axis=0)  138 us
    psum x1, waiting for transfers between devices, on_device(): diag_new = diag_grad - lax.psum(contrib, ('row', 'col'))  126 us
    reduce_scatter x1, waiting for transfers between devices, on_device(): lax.psum_scatter(lax.dot_general(block, col_panel, (((0,), (0,)), ((), ()...  124 us
    another operation x3, other arithmetic, on_device(): jax.scipy.linalg.solve_triangular(lower, reduced.T, lower=True, trans=1)  39.6 us
    dot_general x1, matrix products, on_device(): lax.dot_general(block, col_panel, (((0,), (0,)), ((), ())), preferred_ele...  27.7 us
    dot_general x1, matrix products, on_device(): jnp.dot(block, row_panel, preferred_element_type=jnp.float32)  26.7 us
  transfers between devices with their start and end apart: 5, of which 3 were waited for; matrix products, arithmetic and copies ran while one was open for 19% of the time, Pallas kernels for 0%

profile of v1, /device:TPU:0, one launch (start us, length us, event | category | flops | bytes accessed | tf_op | source)
XLA Modules:
  0.0 546.5 jit_solution(8519087662315249348)
XLA Ops:
  7.2 4.3 stack.2
  11.5 6.4 %all-to-all-start = ((bf16[8,768,512]{2,1,0:T(8,128)(2,1)}), bf16[8,768,512]{2,1,0:T(8,128)(2,1)}, u32[]{:S(2)}, u32[]{:S(2)}) async-start(bf16[8,768,512]{2,1,0:T(8,128)(2,1)} %stack.2), calls=%async_computation.1 | async-start | bytes 12582912 | tf_op jit(solution)/shard_map/all_to_all | solution.py:31
  18.6 138.2 %all-to-all-done = bf16[8,768,512]{2,1,0:T(8,128)(2,1)} async-done(((bf16[8,768,512]{2,1,0:T(8,128)(2,1)}), bf16[8,768,512]{2,1,0:T(8,128)(2,1)}, u32[]{:S(2)}, u32[]{:S(2)}) %all-to-all-start) | async-done | bytes 6291488 | tf_op jit(solution)/shard_map/all_to_all | solution.py:31
  156.9 26.7 %fusion.67 = f32[3072,512]{1,0:T(8,128)} fusion(bf16[3072,6144]{1,0:T(8,128)(2,1)} %bitcast.71, bf16[6144,512]{1,0:T(8,128)(2,1)} %bitcast.2), kind=kOutput, calls=%fused_computation.91 | convolution fusion | flops 19327352832 | bytes 50331648 | tf_op jit(solution)/shard_map/dot_general | solution.py:44
  183.7 27.7 %fusion.66 = f32[6144,512]{1,0:T(8,128)} fusion(bf16[3072,6144]{1,0:T(8,128)(2,1)} %bitcast.72, bf16[3072,512]{1,0:T(8,128)(2,1)} %all-gather.2.cloned.1.call-done), kind=kOutput, calls=%fused_computation.90 | convolution fusion | flops 19327352832 | bytes 53477376 | tf_op jit(solution)/shard_map/dot_general | solution.py:35
  211.5 1.1 copy-done.7
  212.8 8.0 %while.5 = (s32[]{:T(128)}, f32[512,512]{1,0:T(8,128)S(1)}, s32[4,2]{0,1:T(2,128)S(1)}, f32[4,128,128]{2,1,0:T(8,128)S(1)}, s32[]{:T(128)}) while((s32[]{:T(128)}, f32[512,512]{1,0:T(8,128)S(1)}, s32[4,2]{0,1:T(2,128)S(1)}, f32[4,128,128]{2,1,0:T(8,128)S(1)}, s32[]{:T(128)}) %tuple.32), condition=%wide.while_cond.1, body=%wide.while_body.1.sunk | while | flops 2 | bytes 131189 | solution.py:50
  213.4 1.3 bitcast_dynamic-update-slice_fusion.2
  215.4 1.3 bitcast_dynamic-update-slice_fusion.2
  217.4 1.3 bitcast_dynamic-update-slice_fusion.2
  219.4 1.3 bitcast_dynamic-update-slice_fusion.2
  220.7 39.5 %custom-call.7 = f32[4,128,128]{1,2,0:T(8,128)S(1)} custom-call(f32[4,128,128]{2,1,0:T(8,128)S(1)} %get-tuple-element.18), custom_call_target="InvertDiagBlocksLowerTriangular" | custom-call | tf_op jit(solution)/shard_map/jit(_solve_triangular)/triangular_solve | solution.py:50
  260.3 124.1 %reduce-scatter.3.cloned.1.call-done = f32[768,512]{1,0:T(8,128)} async-done(((f32[6144,512]{1,0:T(8,128)}), f32[768,512]{1,0:T(8,128)}) %reduce-scatter.3.cloned.1.call-update) | async-done | bytes 1572880 | tf_op jit(solution)/shard_map/reduce_scatter | solution.py:34
  384.4 2.9 subtract_bitcast_fusion
  389.1 1.4 convolution_subtract_fusion.2
  391.0 2.1 convolution_subtract_fusion
  394.4 2.4 fusion.10
  396.8 1.2 fusion.11
  398.0 1.6 copy.8
  399.6 126.4 %all-reduce.2.cloned.1.call-done = f32[512,512]{1,0:T(8,128)} async-done(((f32[512,512]{1,0:T(8,128)}), f32[512,512]{1,0:T(8,128)}) %all-reduce.2.cloned.1.call-update) | async-done | bytes 1048592 | tf_op jit(solution)/shard_map/psum | solution.py:57
  526.0 3.7 convolution_multiply_fusion
  534.5 1.0 convolution_subtract_fusion.3
  535.9 1.5 convolution_subtract_fusion.7
  538.8 1.2 add_multiply_fusion
  (57 shorter events, 13.4 us)
Async XLA Ops:
  11.5 145.4 %all-to-all-start = ((bf16[8,768,512]{2,1,0:T(8,128)(2,1)}), bf16[8,768,512]{2,1,0:T(8,128)(2,1)}, u32[]{:S(2)}, u32[]{:S(2)}) async-start(bf16[8,768,512]{2,1,0:T(8,128)(2,1)} %stack.2), calls=%async_computation.1 | async-start | bytes 12582912 | tf_op jit(solution)/shard_map/all_to_all | solution.py:31
  17.8 165.9 %all-gather.2.cloned.1.call-start = ((), (), s32[]{:S(2)}) async-start(), calls=%async_computation.3 | async-start | bytes 3932160 | tf_op jit(solution)/shard_map/all_gather | solution.py:28
  18.6 241.7 %reduce-scatter.5.cloned.1.call-start = ((), (), s32[]{:S(2)}) async-start(), calls=%async_computation.5 | async-start | bytes 7864320 | tf_op jit(solution)/shard_map/reduce_scatter | solution.py:43
  183.6 200.7 %reduce-scatter.3.cloned.1.call-start = ((), (), s32[]{:S(2)}) async-start(), calls=%async_computation.4 | async-start | bytes 14155776 | tf_op jit(solution)/shard_map/reduce_scatter | solution.py:34
  211.4 1.2 copy-start.7
  211.4 314.6 %all-reduce.2.cloned.1.call-start = ((), (), s32[]{:S(2)}) async-start(), calls=%async_computation.6 | async-start | bytes 2097152 | tf_op jit(solution)/shard_map/psum | solution.py:57
  260.3 132.8 %copy-start.4 = (f32[4,128,128]{1,2,0:T(8,128)}, f32[4,128,128]{1,2,0:T(8,128)S(1)}, u32[]{:S(2)}) copy-start(f32[4,128,128]{1,2,0:T(8,128)S(1)} %custom-call.7) | copy-start | bytes 786436
  391.0 2.6 copy-start.2
  391.0 3.4 copy-start.3
  393.6 0.8 copy-start.6
  399.6 130.1 %copy-start.5 = (f32[4,128,128]{1,2,0:T(8,128)S(1)}, f32[4,128,128]{1,2,0:T(8,128)}, u32[]{:S(2)}) copy-start(f32[4,128,128]{1,2,0:T(8,128)} %copy-done.4) | copy-start | bytes 786436
  535.9 1.9 copy-start
  537.8 1.0 copy-start.1
Sparse Core Ops, SparseCore 0:
  20.5 45.2 all-gather.1
  183.7 69.1 reduce-scatter.4
  255.2 129.0 reduce-scatter.2
  396.9 129.0 all-reduce.1
